TPU v7x, 128 devices: a whole 4x4x4 slice. The times are simulated.
128 devices in a mesh: seq: 16 (over z_lo, x, core), res: 8 (over y, z_hi).
Axes of the slice: x: 4, y: 4, z: 4 (z_hi: 2, z_lo: 2; z = z_hi * 2 + z_lo), core: 2. Of those that a mesh axis runs over, the one named last changes fastest.
Arguments:
- states: bfloat16 [512, 256, 768], P('seq', 'res'), may hold values from -6 to 6
- row_query: bfloat16 [768, 768], replicated, as said below
- row_key: bfloat16 [768, 768], replicated
- row_value: bfloat16 [768, 768], replicated, may hold values from -0.21875 to 0.21875
- row_out: bfloat16 [768, 768], replicated, may hold values from -0.21875 to 0.21875
- col_query: bfloat16 [768, 768], replicated, as said below
- col_key: bfloat16 [768, 768], replicated
- col_value: bfloat16 [768, 768], replicated, may hold values from -0.21875 to 0.21875
- col_out: bfloat16 [768, 768], replicated, may hold values from -0.21875 to 0.21875
Outputs:
- updated: bfloat16 [512, 256, 768], P('seq', 'res')
Inputs may be any that keep to these rules, and one draw needn't show every extreme that they name: No bound on the size of row_query and row_key entries or of the scores they give is promised. No bound on the size of col_query and col_key entries or of the scores they give is promised.
All inputs are finite; a program needn't handle non-finite values.
Results may differ from a plain program's by a relative error of at most 0.02.
Values may be sent and summed in bfloat16 or wider, within the bound.
A program may use at most 128 MiB of HBM per device.

v0:
```python
import math

import jax
import jax.numpy as jnp
from jax import lax
from jax.sharding import PartitionSpec as P

D = 768
HEADS = 12


def normalize(states):
    values = states.astype(jnp.float32)
    center = values - jnp.mean(values, axis=-1, keepdims=True)
    spread = jnp.mean(center * center, axis=-1, keepdims=True)
    return (center * lax.rsqrt(spread + 1e-05)).astype(jnp.bfloat16)


def project(inputs, weight):
    return jnp.dot(inputs, weight, preferred_element_type=jnp.float32)


def split_heads(field):
    return field.reshape(field.shape[0], field.shape[1], HEADS, D // HEADS)


def on_device(
    states, row_query, row_key, row_value, row_out, col_query, col_key, col_value, col_out
):
    row_count, col_count = (states.shape[0], states.shape[1])
    head_dim = D // HEADS
    all_rows = row_count * lax.axis_size("seq")
    tied_scale = head_dim ** (-0.5) / math.sqrt(all_rows)
    normed = normalize(states)
    q1 = project(normed, row_query).astype(jnp.bfloat16)
    k1 = project(normed, row_key).astype(jnp.bfloat16)
    v1 = project(normed, row_value).astype(jnp.bfloat16)
    q_moved, k_moved, v_moved = (
        lax.all_to_all(q1, "res", split_axis=0, concat_axis=1, tiled=True),
        lax.all_to_all(k1, "res", split_axis=0, concat_axis=1, tiled=True),
        lax.all_to_all(v1, "res", split_axis=0, concat_axis=1, tiled=True),
    )
    partial_value = (
        jnp.einsum(
            "rihd,rjhd->hij",
            split_heads(q_moved),
            split_heads(k_moved),
            preferred_element_type=jnp.float32,
        )
        * tied_scale
    )
    tied = lax.psum(partial_value, ("seq", "res"))
    prob1 = jax.nn.softmax(tied, axis=-1).astype(jnp.bfloat16)
    o_moved = jnp.einsum(
        "hij,rjhd->rihd", prob1, split_heads(v_moved), preferred_element_type=jnp.float32
    ).astype(jnp.bfloat16)
    o_moved = o_moved.reshape(o_moved.shape[0], o_moved.shape[1], D)
    o1 = lax.all_to_all(o_moved, "res", split_axis=1, concat_axis=0, tiled=True)
    mid = (states.astype(jnp.float32) + project(o1, row_out)).astype(jnp.bfloat16)
    normed2 = normalize(mid)
    q2 = project(normed2, col_query).astype(jnp.bfloat16)
    k2 = project(normed2, col_key).astype(jnp.bfloat16)
    v2 = project(normed2, col_value).astype(jnp.bfloat16)
    q_cols, k_cols, v_cols = (
        lax.all_to_all(q2, "seq", split_axis=1, concat_axis=0, tiled=True),
        lax.all_to_all(k2, "seq", split_axis=1, concat_axis=0, tiled=True),
        lax.all_to_all(v2, "seq", split_axis=1, concat_axis=0, tiled=True),
    )
    gathered_rows, local_cols = (q_cols.shape[0], q_cols.shape[1])

    def arrange(field):
        return field.reshape(gathered_rows, local_cols, HEADS, head_dim).transpose(1, 0, 2, 3)

    def attend(triple):
        query_col, key_col, value_col = triple
        score = jnp.einsum(
            "rhd,shd->hrs", query_col, key_col, preferred_element_type=jnp.float32
        ) * head_dim ** (-0.5)
        prob2 = jax.nn.softmax(score, axis=-1).astype(jnp.bfloat16)
        return jnp.einsum(
            "hrs,shd->rhd", prob2, value_col, preferred_element_type=jnp.float32
        ).astype(jnp.bfloat16)

    o2 = lax.map(attend, (arrange(q_cols), arrange(k_cols), arrange(v_cols)))
    o2 = o2.reshape(local_cols, gathered_rows, D).transpose(1, 0, 2)
    colupd = project(o2, col_out).astype(jnp.bfloat16)
    colupd = lax.all_to_all(colupd, "seq", split_axis=0, concat_axis=1, tiled=True)
    return (mid.astype(jnp.float32) + colupd.astype(jnp.float32)).astype(jnp.bfloat16)


def solution(mesh):
    placed = (P("seq", "res", None), P(), P(), P(), P(), P(), P(), P(), P())
    return jax.shard_map(
        on_device, mesh=mesh, in_specs=placed, out_specs=P("seq", "res", None), check_vma=False
    )
```

profile of v0, /device:TPU:1, one launch (start us, length us, event | category | flops | bytes accessed | tf_op | source)
XLA Modules:
  0.0 487.7 jit_solution(7350773890253013936)
XLA Ops:
  11.7 8.3 %all-to-all-start.1 = ((bf16[32,32,768]{2,1,0:T(8,128)(2,1)}), bf16[32,32,768]{2,1,0:T(8,128)(2,1)}, u32[]{:S(2)}, u32[]{:S(2)}) async-start(bf16[32,32,768]{2,1,0:T(8,128)(2,1)} %convolution_convert_fusion.5), calls=%async_computation.1 | async-start | bytes 3145728 | tf_op jit(solution)/shard_map/all_to_all | solution.py:39
  23.9 19.3 %all-to-all-done.1 = bf16[32,32,768]{2,1,0:T(8,128)(2,1)} async-done(((bf16[32,32,768]{2,1,0:T(8,128)(2,1)}), bf16[32,32,768]{2,1,0:T(8,128)(2,1)}, u32[]{:S(2)}, u32[]{:S(2)}) %all-to-all-start.1) | async-done | bytes 1572896 | tf_op jit(solution)/shard_map/all_to_all | solution.py:39
  50.3 5.9 %reshape.63 = bf16[4,256,12,64]{3,2,1,0:T(8,128)(2,1)} reshape(bf16[4,8,32,768]{3,2,1,0:T(8,128)(2,1)} %bitcast.147) | data formatting | bytes 3145728 | tf_op jit(solution)/shard_map/reshape | solution.py:24
  56.2 13.5 %all-to-all-done.2 = bf16[32,32,768]{2,1,0:T(8,128)(2,1)} async-done(((bf16[32,32,768]{2,1,0:T(8,128)(2,1)}), bf16[32,32,768]{2,1,0:T(8,128)(2,1)}, u32[]{:S(2)}, u32[]{:S(2)}) %all-to-all-start.2) | async-done | bytes 1572896 | tf_op jit(solution)/shard_map/all_to_all | solution.py:40
  72.3 5.9 %reshape.64 = bf16[4,256,12,64]{3,2,1,0:T(8,128)(2,1)} reshape(bf16[4,8,32,768]{3,2,1,0:T(8,128)(2,1)} %bitcast.148) | data formatting | bytes 3145728 | tf_op jit(solution)/shard_map/reshape | solution.py:24
  78.2 6.7 %bitcast_multiply_fusion = f32[12,256,256]{2,1,0:T(8,128)} fusion(bf16[4,256,12,64]{3,2,1,0:T(8,128)(2,1)} %reshape.64, bf16[4,256,12,64]{3,2,1,0:T(8,128)(2,1)} %reshape.63), kind=kOutput, calls=%fused_computation.43 | convolution fusion | flops 403439616 | bytes 6291456 | tf_op jit(solution)/shard_map/rihd,rjhd->hij/dot_general | solution.py:44
  87.7 26.8 %all_to_all.117 = bf16[32,32,768]{2,1,0:T(8,128)(2,1)S(1)} all-to-all(bf16[32,32,768]{2,1,0:T(8,128)(2,1)S(1)} %convolution_convert_fusion.6), channel_id=1, replica_groups=mesh['seq'=16,'res'=8] {'res'}, dimensions={0} | all-to-all | bytes 3145728 | tf_op jit(solution)/shard_map/all_to_all | solution.py:41
  115.8 5.9 %reshape.62 = bf16[4,256,12,64]{3,2,1,0:T(8,128)(2,1)} reshape(bf16[4,8,32,768]{3,2,1,0:T(8,128)(2,1)} %bitcast.149) | data formatting | bytes 3145728 | tf_op jit(solution)/shard_map/reshape | solution.py:24
  121.7 123.8 %all-reduce.2.cloned.1.call-done = f32[12,256,256]{2,1,0:T(8,128)} async-done(((f32[12,256,256]{2,1,0:T(8,128)}), f32[12,256,256]{2,1,0:T(8,128)}) %all-reduce.2.cloned.1.call-update) | async-done | bytes 3145744 | tf_op jit(solution)/shard_map/psum | solution.py:52
  249.3 12.5 %fusion.63 = bf16[4,256,12,64]{1,3,0,2:T(8,128)(2,1)} fusion(f32[12,256]{1,0:T(8,128)S(1)} %fusion.92, bf16[4,256,12,64]{3,2,1,0:T(8,128)(2,1)} %reshape.62, f32[12,256,256]{2,1,0:T(8,128)} %all-reduce.2.cloned.1.call-done), kind=kOutput, calls=%fused_computation.68 | convolution fusion | flops 405802240 | bytes 6303744 | tf_op jit(solution)/shard_map/hij,rjhd->rihd/dot_general | solution.py:54
  268.2 25.9 %all_to_all.118 = bf16[4,256,768]{2,0,1:T(4,128)(2,1)S(1)} all-to-all(bf16[4,256,768]{2,0,1:T(4,128)(2,1)} %copy.42), channel_id=1, replica_groups=mesh['seq'=16,'res'=8] {'res'}, dimensions={1} | all-to-all | bytes 3145728 | tf_op jit(solution)/shard_map/all_to_all | solution.py:58
  301.3 6.3 %all-to-all-start.6 = ((bf16[32,32,768]{2,0,1:T(8,128)(2,1)}), bf16[32,32,768]{2,0,1:T(8,128)(2,1)S(1)}, u32[]{:S(2)}, u32[]{:S(2)}) async-start(bf16[32,32,768]{2,0,1:T(8,128)(2,1)} %copy.49), calls=%async_computation.6 | async-start | bytes 3145728 | tf_op jit(solution)/shard_map/all_to_all | solution.py:66
  312.9 16.3 %all-to-all-done.6 = bf16[32,32,768]{2,0,1:T(8,128)(2,1)S(1)} async-done(((bf16[32,32,768]{2,0,1:T(8,128)(2,1)}), bf16[32,32,768]{2,0,1:T(8,128)(2,1)S(1)}, u32[]{:S(2)}, u32[]{:S(2)}) %all-to-all-start.6) | async-done | bytes 1572896 | tf_op jit(solution)/shard_map/all_to_all | solution.py:66
  339.3 16.4 %all-to-all-done.5 = bf16[32,32,768]{2,0,1:T(8,128)(2,1)} async-done(((bf16[32,32,768]{2,0,1:T(8,128)(2,1)}), bf16[32,32,768]{2,0,1:T(8,128)(2,1)}, u32[]{:S(2)}, u32[]{:S(2)}) %all-to-all-start.5) | async-done | bytes 1572896 | tf_op jit(solution)/shard_map/all_to_all | solution.py:65
  355.7 13.4 %all-to-all-start.4 = ((bf16[32,32,768]{2,0,1:T(8,128)(2,1)}), bf16[32,32,768]{2,0,1:T(8,128)(2,1)}, u32[]{:S(2)}, u32[]{:S(2)}) async-start(bf16[32,32,768]{2,0,1:T(8,128)(2,1)} %copy.45), calls=%async_computation.4 | async-start | bytes 3145728 | tf_op jit(solution)/shard_map/all_to_all | solution.py:67
  370.4 5.9 %reshape.68 = bf16[512,2,12,64]{3,2,0,1:T(8,128)(2,1)} reshape(bf16[16,32,2,768]{3,1,0,2:T(8,128)(2,1)} %bitcast.150) | data formatting | bytes 3145728 | tf_op jit(solution)/shard_map/reshape | solution.py:72
  397.8 5.5 %copy.51 = bf16[2,512,12,64]{1,3,2,0:T(8,128)(2,1)} copy(bf16[2,512,12,64]{3,2,1,0:T(8,128)(2,1)} %bitcast.142) | data formatting | bytes 3145728 | tf_op jit(solution)/shard_map/while | solution.py:84
  403.2 32.3 %while.10 = (s32[]{:T(128)}, bf16[2,512,12,64]{1,3,2,0:T(8,128)(2,1)S(1)}, bf16[2,512,12,64]{1,3,2,0:T(8,128)(2,1)}, bf16[2,512,12,64]{1,3,2,0:T(8,128)(2,1)}, bf16[2,512,12,64]{1,3,2,0:T(8,128)(2,1)}, /*index=5*/s32[]{:T(128)}) while((s32[]{:T(128)}, bf16[2,512,12,64]{1,3,2,0:T(8,128)(2,1)S(1)}, bf16[2,512,12,64]{1,3,2,0:T(8,128)(2,1)}, ...), condition=%wide.region_10.11_spmd, body=%wide.region_7.10_spmd.sunk | while | flops 821428736 | bytes 28371012 | solution.py:84
  403.2 10.1 %fusion.105 = (f32[12,512]{1,0:T(8,128)S(1)}, f32[12,512,512]{1,2,0:T(8,128)}) fusion(bf16[2,512,12,64]{1,3,2,0:T(8,128)(2,1)} %get-tuple-element.108, s32[]{:T(128)} %get-tuple-element.98, bf16[2,512,12,64]{1,3,2,0:T(8,128)(2,1)} %get-tuple-element.107), kind=kOutput, calls=%fused_computation.82.clone.1 | convolution fusion | flops 412090880 | bytes 14181376 | tf_op jit(solution)/shard_map/while/body/eval_jaxpr/sub | solution.py:79
  413.3 6.0 %fusion.106 = bf16[2,512,12,64]{1,3,2,0:T(8,128)(2,1)S(1)} fusion(bf16[2,512,12,64]{1,3,2,0:T(8,128)(2,1)S(1)} %get-tuple-element.99, s32[]{:T(128)} %get-tuple-element.98, f32[12,512,512]{1,2,0:T(8,128)} %get-tuple-element.90, f32[12,512]{1,0:T(8,128)S(1)} %get-tuple-element.91, bf16[2,512,12,64]{1,3,2,0:T(8,128)(2,1)} %get-tuple-element.106), kind=kOutput, calls=%fused_computation.10.clone.1 | convolution fusion | flops 409337856 | bytes 14189568 | tf_op jit(solution)/shard_map/while/body/eval_jaxpr/hrs,shd->rhd/dot_general | solution.py:80
  419.4 10.1 %fusion.105 = (f32[12,512]{1,0:T(8,128)S(1)}, f32[12,512,512]{1,2,0:T(8,128)}) fusion(bf16[2,512,12,64]{1,3,2,0:T(8,128)(2,1)} %get-tuple-element.108, s32[]{:T(128)} %get-tuple-element.98, bf16[2,512,12,64]{1,3,2,0:T(8,128)(2,1)} %get-tuple-element.107), kind=kOutput, calls=%fused_computation.82.clone.1 | convolution fusion | flops 412090880 | bytes 14181376 | tf_op jit(solution)/shard_map/while/body/eval_jaxpr/sub | solution.py:79
  429.4 6.0 %fusion.106 = bf16[2,512,12,64]{1,3,2,0:T(8,128)(2,1)S(1)} fusion(bf16[2,512,12,64]{1,3,2,0:T(8,128)(2,1)S(1)} %get-tuple-element.99, s32[]{:T(128)} %get-tuple-element.98, f32[12,512,512]{1,2,0:T(8,128)} %get-tuple-element.90, f32[12,512]{1,0:T(8,128)S(1)} %get-tuple-element.91, bf16[2,512,12,64]{1,3,2,0:T(8,128)(2,1)} %get-tuple-element.106), kind=kOutput, calls=%fused_computation.10.clone.1 | convolution fusion | flops 409337856 | bytes 14189568 | tf_op jit(solution)/shard_map/while/body/eval_jaxpr/hrs,shd->rhd/dot_general | solution.py:80
  441.5 26.7 %all_to_all.119 = bf16[512,2,768]{2,1,0:T(2,128)(2,1)S(1)} all-to-all(bf16[512,2,768]{2,1,0:T(2,128)(2,1)S(1)} %copy.55), channel_id=1, replica_groups=mesh['seq'=16,'res'=8] {'seq'}, dimensions={0} | all-to-all | bytes 3145728 | tf_op jit(solution)/shard_map/all_to_all | solution.py:87
  471.6 5.4 %reshape.70 = f32[32,32,768]{2,1,0:T(8,128)} reshape(f32[32,16,2,768]{3,2,1,0:T(2,128)} %copy_bitcast_fusion) | data formatting | bytes 6291456 | tf_op jit(solution)/shard_map/convert_element_type | solution.py:88
  (61 shorter events, 91.2 us)
Async XLA Ops:
  6.5 287.9 %copy-start = (bf16[768,768]{1,0:T(8,128)(2,1)S(1)}, bf16[768,768]{1,0:T(8,128)(2,1)}, u32[]{:S(2)}) copy-start(bf16[768,768]{1,0:T(8,128)(2,1)} %param.15) | copy-start | bytes 3538948
  6.5 2.0 copy-start.2
  6.5 2.6 copy-start.6
  11.7 31.5 %all-to-all-start.1 = ((bf16[32,32,768]{2,1,0:T(8,128)(2,1)}), bf16[32,32,768]{2,1,0:T(8,128)(2,1)}, u32[]{:S(2)}, u32[]{:S(2)}) async-start(bf16[32,32,768]{2,1,0:T(8,128)(2,1)} %convolution_convert_fusion.5), calls=%async_computation.1 | async-start | bytes 3145728 | tf_op jit(solution)/shard_map/all_to_all | solution.py:39
  43.2 26.4 %all-to-all-start.2 = ((bf16[32,32,768]{2,1,0:T(8,128)(2,1)}), bf16[32,32,768]{2,1,0:T(8,128)(2,1)}, u32[]{:S(2)}, u32[]{:S(2)}) async-start(bf16[32,32,768]{2,1,0:T(8,128)(2,1)} %convolution_convert_fusion.4), calls=%async_computation.2 | async-start | bytes 3145728 | tf_op jit(solution)/shard_map/all_to_all | solution.py:40
  47.5 198.0 %all-reduce.2.cloned.1.call-start = ((), (), s32[]{:S(2)}) async-start(), calls=%async_computation.8 | async-start | bytes 6291456 | tf_op jit(solution)/shard_map/psum | solution.py:52
  295.9 3.4 copy-start.3
  296.0 1.8 copy-start.7
  301.3 27.8 %all-to-all-start.6 = ((bf16[32,32,768]{2,0,1:T(8,128)(2,1)}), bf16[32,32,768]{2,0,1:T(8,128)(2,1)S(1)}, u32[]{:S(2)}, u32[]{:S(2)}) async-start(bf16[32,32,768]{2,0,1:T(8,128)(2,1)} %copy.49), calls=%async_computation.6 | async-start | bytes 3145728 | tf_op jit(solution)/shard_map/all_to_all | solution.py:66
  329.1 26.5 %all-to-all-start.5 = ((bf16[32,32,768]{2,0,1:T(8,128)(2,1)}), bf16[32,32,768]{2,0,1:T(8,128)(2,1)}, u32[]{:S(2)}, u32[]{:S(2)}) async-start(bf16[32,32,768]{2,0,1:T(8,128)(2,1)} %copy.47), calls=%async_computation.5 | async-start | bytes 3145728 | tf_op jit(solution)/shard_map/all_to_all | solution.py:65
  355.7 36.7 %all-to-all-start.4 = ((bf16[32,32,768]{2,0,1:T(8,128)(2,1)}), bf16[32,32,768]{2,0,1:T(8,128)(2,1)}, u32[]{:S(2)}, u32[]{:S(2)}) async-start(bf16[32,32,768]{2,0,1:T(8,128)(2,1)} %copy.45), calls=%async_computation.4 | async-start | bytes 3145728 | tf_op jit(solution)/shard_map/all_to_all | solution.py:67
  397.8 5.5 %copy-start.5 = (bf16[2,512,12,64]{1,3,2,0:T(8,128)(2,1)S(1)}, bf16[2,512,12,64]{1,3,2,0:T(8,128)(2,1)}, u32[]{:S(2)}) copy-start(bf16[2,512,12,64]{1,3,2,0:T(8,128)(2,1)} %custom-call) | copy-start | bytes 4718596
  435.5 1.6 copy-start.8
  471.6 5.4 %copy-start.4 = (bf16[32,32,768]{2,1,0:T(8,128)(2,1)S(1)}, bf16[32,32,768]{2,1,0:T(8,128)(2,1)}, u32[]{:S(2)}) copy-start(bf16[32,32,768]{2,1,0:T(8,128)(2,1)} %copy-done.3) | copy-start | bytes 4718596
  477.0 3.6 copy-start.1
Sparse Core Ops, SparseCore 0:
  85.1 160.3 all-reduce.1
where the time goes:
time: 496 us; the launch traced here: 488 us
  waiting for transfers between devices  189 us (38%)
  local copies, waits for them, and re-layouts  81.2 us (16%)
  blocking collectives  79.4 us (16%)
  matrix products  72.8 us (15%)
  starting transfers between devices  37.3 us (8%)
  between operations  13.9 us (3%)
  other arithmetic  13.8 us (3%)
    psum x1, waiting for transfers between devices, on_device(): tied = lax.psum(partial_value, ('seq', 'res'))  124 us
    all_to_all x1, blocking collectives, on_device(): lax.all_to_all(v1, 'res', split_axis=0, concat_axis=1, tiled=True)  26.8 us
    all_to_all x1, blocking collectives, on_device(): lax.all_to_all(colupd, 'seq', split_axis=0, concat_axis=1, tiled=True)  26.7 us
    all_to_all x1, blocking collectives, on_device(): o1 = lax.all_to_all(o_moved, 'res', split_axis=1, concat_axis=0, tiled=True)  25.9 us
    dot_general x8, matrix products, project(): return jnp.dot(inputs, weight, preferred_element_type=jnp.float32)  21.4 us
    sub x2, matrix products, attend(): prob2 = jax.nn.softmax(score, axis=-1).astype(jnp.bfloat16)  20.1 us
    all_to_all x1, waiting for transfers between devices, on_device(): lax.all_to_all(q1, 'res', split_axis=0, concat_axis=1, tiled=True)  19.3 us
    reshape x3, local copies, waits for them, and re-layouts, split_heads(): return field.reshape(field.shape[0], field.shape[1], HEADS, D // HEADS)  17.7 us
  transfers between devices with their start and end apart: 6, of which 5 were waited for; matrix products, arithmetic and copies ran while one was open for 11% of the time, Pallas kernels for 0%

commit v1 on v0

v1 whole, which is shorter than its diff:
```python
import math

import jax
import jax.numpy as jnp
from jax import lax
from jax.sharding import PartitionSpec as P

D = 768
HEADS = 12
HD = D // HEADS


def normalize(states):
    values = states.astype(jnp.float32)
    center = values - jnp.mean(values, axis=-1, keepdims=True)
    spread = jnp.mean(center * center, axis=-1, keepdims=True)
    return (center * lax.rsqrt(spread + 1e-05)).astype(jnp.bfloat16)


def project(inputs, weight):
    return jnp.dot(inputs, weight, preferred_element_type=jnp.float32)


def on_device(
    states, row_query, row_key, row_value, row_out, col_query, col_key, col_value, col_out
):
    rows, cols = states.shape[0], states.shape[1]
    seq, res = lax.axis_size("seq"), lax.axis_size("res")
    own_rows, own_cols = rows // res, cols // seq
    all_rows, all_cols = rows * seq, cols * res
    tied_scale = HD ** (-0.5) / math.sqrt(all_rows)
    moved = lax.all_to_all(
        states.reshape(res, own_rows, cols, D), "res", split_axis=0, concat_axis=0
    )
    by_row = moved.transpose(1, 0, 2, 3).reshape(own_rows, all_cols, D)
    normed = normalize(by_row)
    q1 = project(normed, row_query).astype(jnp.bfloat16).reshape(own_rows, all_cols, HEADS, HD)
    k1 = project(normed, row_key).astype(jnp.bfloat16).reshape(own_rows, all_cols, HEADS, HD)
    v1 = project(normed, row_value).astype(jnp.bfloat16).reshape(own_rows, all_cols, HEADS, HD)
    part = jnp.einsum("rihd,rjhd->hij", q1, k1, preferred_element_type=jnp.float32) * tied_scale
    part = part.reshape(HEADS * all_cols, all_cols)
    tied = lax.psum_scatter(part, ("seq", "res"), scatter_dimension=0, tiled=True)
    prob1 = jax.nn.softmax(tied, axis=-1).astype(jnp.bfloat16)
    prob1 = lax.all_gather(prob1, ("seq", "res"), axis=0, tiled=True)
    prob1 = prob1.reshape(HEADS, all_cols, all_cols)
    o1 = jnp.einsum("hij,rjhd->rihd", prob1, v1, preferred_element_type=jnp.float32)
    o1 = o1.astype(jnp.bfloat16).reshape(own_rows, all_cols, D)
    mid = (by_row.astype(jnp.float32) + project(o1, row_out)).astype(jnp.bfloat16)
    mid = mid.reshape(own_rows, res, seq, own_cols, D).transpose(2, 1, 0, 3, 4)
    mid = mid.reshape(seq * res, own_rows, own_cols, D)
    mid = lax.all_to_all(mid, ("seq", "res"), split_axis=0, concat_axis=0)
    mid = mid.reshape(all_rows, own_cols, D).transpose(1, 0, 2)
    normed2 = normalize(mid)
    q2 = project(normed2, col_query).astype(jnp.bfloat16).reshape(own_cols, all_rows, HEADS, HD)
    k2 = project(normed2, col_key).astype(jnp.bfloat16).reshape(own_cols, all_rows, HEADS, HD)
    v2 = project(normed2, col_value).astype(jnp.bfloat16).reshape(own_cols, all_rows, HEADS, HD)
    score = jnp.einsum("crhd,cshd->chrs", q2, k2, preferred_element_type=jnp.float32)
    prob2 = jax.nn.softmax(score * HD ** (-0.5), axis=-1).astype(jnp.bfloat16)
    o2 = jnp.einsum("chrs,cshd->crhd", prob2, v2, preferred_element_type=jnp.float32)
    o2 = o2.astype(jnp.bfloat16).reshape(own_cols, all_rows, D)
    colupd = project(o2, col_out).astype(jnp.bfloat16)
    updated = (mid.astype(jnp.float32) + colupd.astype(jnp.float32)).astype(jnp.bfloat16)
    updated = updated.reshape(own_cols, seq, rows, D).transpose(1, 2, 0, 3)
    updated = lax.all_to_all(updated, "seq", split_axis=0, concat_axis=0)
    return updated.transpose(1, 0, 2, 3).reshape(rows, cols, D)


def solution(mesh):
    placed = (P("seq", "res", None), P(), P(), P(), P(), P(), P(), P(), P())
    return jax.shard_map(
        on_device, mesh=mesh, in_specs=placed, out_specs=P("seq", "res", None), check_vma=False
    )
```

time: 496 us -> 1120 us (2.26)
  waiting for transfers between devices: 189 us -> 933 us
  local copies, waits for them, and re-layouts: 81.2 us -> 24.6 us
  starting transfers between devices: 37.3 us -> 0.22 us
  matrix products: 72.8 us -> 50.5 us
    reduce_scatter x0 -> x1, waiting for transfers between devices: none -> 633 us  [on_device(): lax.psum_scatter(part, ('seq', 'res'), scatter_dimension=0, tiled=True)]
    all_gather x0 -> x1, waiting for transfers between devices: none -> 300 us  [on_device(): prob1 = lax.all_gather(prob1, ('seq', 'res'), axis=0, tiled=True)]
    psum x1 -> x0, waiting for transfers between devices: 124 us -> none  [on_device(): tied = lax.psum(partial_value, ('seq', 'res'))]
    all_to_all x5 -> x0, waiting for transfers between devices: 65.5 us -> none  [the longest x1 19.3 us: on_device(): lax.all_to_all(q1, 'res', split_axis=0, concat_axis=1, tiled=True)]
    all_to_all x5 -> x0, starting transfers between devices: 37.3 us -> none  [the longest x1 13.4 us: on_device(): lax.all_to_all(v2, 'seq', split_axis=1, concat_axis=0, tiled=True)]
    reshape x8 -> x5, local copies, waits for them, and re-layouts: 36.6 us -> 5.25 us  [the longest x1 2.01 us: on_device(): return updated.transpose(1, 0, 2, 3).reshape(rows, cols, D)]
    while x3 -> x0, local copies, waits for them, and re-layouts: 16.1 us -> none  [on_device(): o2 = lax.map(attend, (arrange(q_cols), arrange(k_cols), arrange(v_cols)))]
    dot_general x4 -> x3, matrix products: 31.3 us -> 15.5 us  [the longest x1 11 us: on_device(): jnp.einsum('chrs,cshd->crhd', prob2, v2, preferred_element_type=jnp.float32)]
  transfers between devices with their start and end apart: 6 -> 2, of which waited for: 5 -> 2; matrix products, arithmetic and copies ran while one was open for 11% -> 0% of each run, Pallas kernels for 0% -> 0%
where the time goes in v1:
time: 1120 us; the launch traced here: 1110 us
  waiting for transfers between devices  933 us (83%)
  blocking collectives  86.4 us (8%)
  matrix products  50.5 us (5%)
  local copies, waits for them, and re-layouts  24.6 us (2%)
  between operations  13.6 us (1%)
    reduce_scatter x1, waiting for transfers between devices, on_device(): lax.psum_scatter(part, ('seq', 'res'), scatter_dimension=0, tiled=True)  633 us
    all_gather x1, waiting for transfers between devices, on_device(): prob1 = lax.all_gather(prob1, ('seq', 'res'), axis=0, tiled=True)  300 us
    all_to_all x1, blocking collectives, on_device(): mid = lax.all_to_all(mid, ('seq', 'res'), split_axis=0, concat_axis=0)  31.3 us
    all_to_all x1, blocking collectives, on_device(): lax.all_to_all(states.reshape(res, own_rows, cols, D), 'res', split_axis=...  29.4 us
    all_to_all x1, blocking collectives, on_device(): updated = lax.all_to_all(updated, 'seq', split_axis=0, concat_axis=0)  25.8 us
  transfers between devices with their start and end apart: 2, of which 2 were waited for; matrix products, arithmetic and copies ran while one was open for 0% of the time, Pallas kernels for 0%

profile of v1, /device:TPU:1, one launch (start us, length us, event | category | flops | bytes accessed | tf_op | source)
XLA Modules:
  0.0 1114.7 jit_solution(17327529294043333661)
XLA Ops:
  6.5 29.4 %all_to_all.15 = bf16[8,4,32,768]{3,2,1,0:T(8,128)(2,1)S(1)} all-to-all(bf16[8,4,32,768]{3,2,1,0:T(8,128)(2,1)} %bitcast.110), channel_id=1, replica_groups=mesh['seq'=16,'res'=8] {'res'}, dimensions={0} | all-to-all | bytes 3145728 | tf_op jit(solution)/shard_map/all_to_all | solution.py:32
  42.6 4.3 convolution_convert_fusion.6
  46.9 1.7 copy.99
  48.6 2.3 bitcast_multiply_fusion
  51.2 633.3 %reduce-scatter.2.cloned.1.call-done = f32[24,256]{1,0:T(8,128)} async-done(((f32[3072,256]{1,0:T(8,128)}), f32[24,256]{1,0:T(8,128)}) %reduce-scatter.2.cloned.1.call-update) | async-done | bytes 24592 | tf_op jit(solution)/shard_map/reduce_scatter | solution.py:42
  687.8 2.7 convolution_convert_fusion.7
  691.1 299.8 %all-gather.2.cloned.1.call-done = bf16[3072,256]{1,0:T(8,128)(2,1)} async-done(((bf16[24,256]{1,0:T(8,128)(2,1)}), bf16[3072,256]{1,0:T(8,128)(2,1)}) %all-gather.2.cloned.1.call-update) | async-done | bytes 1572880 | tf_op jit(solution)/shard_map/all_gather | solution.py:44
  990.9 2.1 fusion.15
  993.2 1.7 copy-done.3
  994.9 1.5 fusion.11
  998.0 1.6 copy.105
  999.6 31.3 %all_to_all.16 = bf16[128,4,2,768]{3,2,1,0:T(2,128)(2,1)S(1)} all-to-all(bf16[128,4,2,768]{3,2,1,0:T(2,128)(2,1)S(1)} %copy.105), channel_id=1, replica_groups=mesh['seq'=16,'res'=8] {'seq','res'}, dimensions={0} | all-to-all | bytes 3145728 | tf_op jit(solution)/shard_map/all_to_all | solution.py:51
  1031.2 2.4 copy.107
  1035.9 2.6 convolution_convert_fusion.1
  1038.5 2.6 copy.111
  1041.1 4.4 convolution_convert_fusion.2
  1045.5 2.5 convolution_convert_fusion.3
  1048.1 2.6 copy.109
  1050.7 2.6 copy.110
  1053.3 14.2 %fusion.30 = (f32[2,12,512]{2,1,0:T(8,128)S(1)}, f32[2,12,512,512]{2,3,1,0:T(8,128)}) fusion(bf16[2,512,12,64]{1,3,2,0:T(8,128)(2,1)} %bitcast.113, bf16[2,512,12,64]{1,3,2,0:T(8,128)(2,1)} %bitcast.111), kind=kOutput, calls=%fused_computation.55 | convolution fusion | flops 824181248 | bytes 28360704 | tf_op jit(solution)/shard_map/sub | solution.py:58
  1067.5 11.0 fusion.12
  1078.5 1.4 fusion.8
  1080.1 25.8 %all_to_all.17 = bf16[16,32,2,768]{3,1,2,0:T(8,128)(2,1)S(1)} all-to-all(bf16[16,32,2,768]{3,1,2,0:T(8,128)(2,1)S(1)} %bitcast.105), channel_id=1, replica_groups=mesh['seq'=16,'res'=8] {'seq'}, dimensions={0} | all-to-all | bytes 3145728 | tf_op jit(solution)/shard_map/all_to_all | solution.py:64
  1105.9 2.0 copy.115
  (53 shorter events, 15.2 us)
Async XLA Ops:
  6.5 34.0 %copy-start = (bf16[768,768]{1,0:T(8,128)(2,1)S(1)}, bf16[768,768]{1,0:T(8,128)(2,1)}, u32[]{:S(2)}) copy-start(bf16[768,768]{1,0:T(8,128)(2,1)} %param.11) | copy-start | bytes 3538948
  6.5 678.0 %reduce-scatter.2.cloned.1.call-start = ((), (), s32[]{:S(2)}) async-start(), calls=%async_computation.4 | async-start | bytes 3170304 | tf_op jit(solution)/shard_map/reduce_scatter | solution.py:42
  37.7 1.7 copy-start.2
  39.4 1.1 copy-start.4
  50.9 636.8 %copy-start.5 = (bf16[4,256,768]{2,1,0:T(8,128)(2,1)S(1)}, bf16[4,256,768]{2,1,0:T(8,128)(2,1)}, u32[]{:S(2)}) copy-start(bf16[4,256,768]{2,1,0:T(8,128)(2,1)} %copy-done.4) | copy-start | bytes 4718596
  51.0 940.0 %all-gather.2.cloned.1.call-start = ((), (), s32[]{:S(2)}) async-start(), calls=%async_computation.5 | async-start | bytes 1585152 | tf_op jit(solution)/shard_map/all_gather | solution.py:44
  990.9 2.3 copy-start.8
  993.0 1.9 copy-start.3
  1034.4 1.5 copy-start.9
  1034.7 1.1 copy-start.6
  1041.1 4.4 copy-start.7
  1041.1 4.4 copy-start.10
  1067.5 11.0 copy-start.11
  1105.9 2.0 copy-start.1
Sparse Core Ops, SparseCore 0:
  51.1 633.3 reduce-scatter.1
  687.9 303.0 all-gather.1

commit v2 on v1

--- a/solution.py
+++ b/solution.py
@@ -1,13 +1,17 @@
+import functools
 import math
 
 import jax
 import jax.numpy as jnp
 from jax import lax
+from jax.experimental import pallas as pl
+from jax.experimental.pallas import tpu as pltpu
 from jax.sharding import PartitionSpec as P
 
 D = 768
 HEADS = 12
 HD = D // HEADS
+MESH = pl.DeviceIdType.MESH
 
 
 def normalize(states):
@@ -19,6 +23,115 @@
 
 def project(inputs, weight):
     return jnp.dot(inputs, weight, preferred_element_type=jnp.float32)
+
+
+def tied_softmax_kernel(scale, part, prob, pair_in, pair_sum, chunk_in, chunk_out,
+                        pair_send, pair_recv, chunk_send, chunk_recv,
+                        prob_send, prob_recv, half_send, half_recv):
+    seq, res = lax.axis_index("seq"), lax.axis_index("res")
+    core, me = seq % 2, (seq // 2) * 8 + res
+    partner = {"seq": seq + 1 - 2 * core, "res": res}
+    mine, other = 6 * core, 6 * (1 - core)
+
+    def chip(m):
+        return {"seq": 2 * (m // 8) + core, "res": m % 8}
+
+    barrier = pltpu.get_barrier_semaphore()
+
+    @pl.loop(1, 64)
+    def _(k):
+        pl.semaphore_signal(barrier, inc=1, device_id=chip((me + k) % 64), device_id_type=MESH)
+
+    pl.semaphore_signal(barrier, inc=1, device_id=partner, device_id_type=MESH)
+    pl.semaphore_wait(barrier, 64)
+
+    def pair_copy(h):
+        return pltpu.make_async_remote_copy(
+            src_ref=part.at[other + h], dst_ref=pair_in.at[h], send_sem=pair_send.at[h],
+            recv_sem=pair_recv.at[h], device_id=partner, device_id_type=MESH)
+
+    def chunk_copy(m, slot):
+        return pltpu.make_async_remote_copy(
+            src_ref=pair_sum.at[pl.ds(3 * (m // 32), 3), m % 32], dst_ref=chunk_in.at[slot],
+            send_sem=chunk_send.at[m], recv_sem=chunk_recv.at[slot],
+            device_id=chip(m), device_id_type=MESH)
+
+    def prob_copy(m, owner):
+        return pltpu.make_async_remote_copy(
+            src_ref=chunk_out, dst_ref=prob.at[pl.ds(mine + 3 * (owner // 32), 3), owner % 32],
+            send_sem=prob_send.at[m], recv_sem=prob_recv.at[owner],
+            device_id=chip(m), device_id_type=MESH)
+
+    @pl.loop(0, 6)
+    def _(h):
+        pair_copy(h).start()
+
+    @pl.loop(0, 6)
+    def _(h):
+        pair_copy(h).wait_recv()
+        pair_sum[h] = part[mine + h] + pair_in[h]
+
+    @pl.loop(1, 64)
+    def _(k):
+        chunk_copy((me + k) % 64, me).start()
+
+    def add(k, total):
+        source = (me + k) % 64
+        chunk_copy(source, source).wait_recv()
+        return total + chunk_in[source]
+
+    total = lax.fori_loop(1, 64, add, pair_sum[pl.ds(3 * (me // 32), 3), me % 32]) * scale
+    total = jnp.exp(total - jnp.max(total, axis=-1, keepdims=True))
+    total = (total / jnp.sum(total, axis=-1, keepdims=True)).astype(jnp.bfloat16)
+    chunk_out[...] = total
+    prob[pl.ds(mine + 3 * (me // 32), 3), me % 32] = total
+
+    @pl.loop(1, 64)
+    def _(k):
+        prob_copy((me + k) % 64, me).start()
+
+    @pl.loop(1, 64)
+    def _(k):
+        source = (me + k) % 64
+        prob_copy(source, source).wait_recv()
+
+    def half_copy(base):
+        return pltpu.make_async_remote_copy(
+            src_ref=prob.at[pl.ds(mine, 6)], dst_ref=prob.at[pl.ds(base, 6)],
+            send_sem=half_send, recv_sem=half_recv, device_id=partner, device_id_type=MESH)
+
+    half_copy(mine).start()
+    half_copy(other).wait_recv()
+
+    @pl.loop(1, 64)
+    def _(k):
+        source = (me + k) % 64
+        chunk_copy(source, me).wait_send()
+        prob_copy(source, me).wait_send()
+
+    @pl.loop(0, 6)
+    def _(h):
+        pair_copy(h).wait_send()
+
+    half_copy(mine).wait_send()
+
+
+def tied_softmax(part, scale):
+    dma = pltpu.SemaphoreType.DMA
+    return pl.pallas_call(
+        functools.partial(tied_softmax_kernel, scale),
+        out_shape=jax.ShapeDtypeStruct((12, 32, 8, 256), jnp.bfloat16),
+        in_specs=[pl.BlockSpec(memory_space=pltpu.VMEM)],
+        out_specs=pl.BlockSpec(memory_space=pltpu.VMEM),
+        scratch_shapes=[
+            pltpu.VMEM((6, 32, 8, 256), jnp.float32),
+            pltpu.VMEM((6, 32, 8, 256), jnp.float32),
+            pltpu.VMEM((64, 3, 8, 256), jnp.float32),
+            pltpu.VMEM((3, 8, 256), jnp.bfloat16),
+            dma((6,)), dma((6,)), dma((64,)), dma((64,)), dma((64,)), dma((64,)), dma, dma,
+        ],
+        compiler_params=pltpu.CompilerParams(collective_id=0, has_side_effects=True),
+    )(part)
 
 
 def on_device(
@@ -37,11 +150,9 @@
     q1 = project(normed, row_query).astype(jnp.bfloat16).reshape(own_rows, all_cols, HEADS, HD)
     k1 = project(normed, row_key).astype(jnp.bfloat16).reshape(own_rows, all_cols, HEADS, HD)
     v1 = project(normed, row_value).astype(jnp.bfloat16).reshape(own_rows, all_cols, HEADS, HD)
-    part = jnp.einsum("rihd,rjhd->hij", q1, k1, preferred_element_type=jnp.float32) * tied_scale
-    part = part.reshape(HEADS * all_cols, all_cols)
-    tied = lax.psum_scatter(part, ("seq", "res"), scatter_dimension=0, tiled=True)
-    prob1 = jax.nn.softmax(tied, axis=-1).astype(jnp.bfloat16)
-    prob1 = lax.all_gather(prob1, ("seq", "res"), axis=0, tiled=True)
+    part = jnp.einsum("rihd,rjhd->hij", q1, k1, preferred_element_type=jnp.float32)
+    part = part.reshape(HEADS, 32, 8, all_cols)
+    prob1 = tied_softmax(part, tied_scale)
     prob1 = prob1.reshape(HEADS, all_cols, all_cols)
     o1 = jnp.einsum("hij,rjhd->rihd", prob1, v1, preferred_element_type=jnp.float32)
     o1 = o1.astype(jnp.bfloat16).reshape(own_rows, all_cols, D)

time: 1120 us -> 220 us (0.20)
  waiting for transfers between devices: 933 us -> 0 us
  Pallas kernels: 0 us -> 52.7 us
  between operations: 13.6 us -> 0.24 us
    reduce_scatter x1 -> x0, waiting for transfers between devices: 633 us -> none  [on_device(): lax.psum_scatter(part, ('seq', 'res'), scatter_dimension=0, tiled=True)]
    all_gather x1 -> x0, waiting for transfers between devices: 300 us -> none  [on_device(): prob1 = lax.all_gather(prob1, ('seq', 'res'), axis=0, tiled=True)]
    pallas_call x0 -> x1, Pallas kernels: none -> 52.7 us  [tied_softmax(): pl.pallas_call(functools.partial(tied_softmax_kernel, scale), out_shape=j...]
  transfers between devices with their start and end apart: 2 -> 0, of which waited for: 2 -> 0; matrix products, arithmetic and copies ran while one was open for 0% -> 0% of each run, Pallas kernels for 0% -> 0%
where the time goes in v2:
time: 220 us
  blocking collectives  85.1 us (39%)
  Pallas kernels  52.7 us (24%)
  matrix products  51.9 us (24%)
  local copies, waits for them, and re-layouts  26.6 us (12%)
  other arithmetic  3.05 us (1%)
    pallas_call x1, Pallas kernels, tied_softmax(): pl.pallas_call(functools.partial(tied_softmax_kernel, scale), out_shape=j...  52.7 us
    all_to_all x1, blocking collectives, on_device(): mid = lax.all_to_all(mid, ('seq', 'res'), split_axis=0, concat_axis=0)  29.9 us
    all_to_all x1, blocking collectives, on_device(): lax.all_to_all(states.reshape(res, own_rows, cols, D), 'res', split_axis=...  29.4 us
    all_to_all x1, blocking collectives, on_device(): updated = lax.all_to_all(updated, 'seq', split_axis=0, concat_axis=0)  25.8 us
    dot_general x8, matrix products, project(): return jnp.dot(inputs, weight, preferred_element_type=jnp.float32)  20.8 us
    sub x1, matrix products, on_device(): prob2 = jax.nn.softmax(score * HD ** (-0.5), axis=-1).astype(jnp.bfloat16)  14.2 us
    dot_general x1, matrix products, on_device(): jnp.einsum('chrs,cshd->crhd', prob2, v2, preferred_element_type=jnp.float32)  11 us
    unnamed x26, local copies, waits for them, and re-layouts  5.32 us

profile of v2, /device:TPU:1, one launch (start us, length us, event | category | flops | bytes accessed | tf_op | source)
XLA Modules:
  0.0 219.6 jit_solution(16217765845479145680)
XLA Ops:
  0.0 29.4 %all_to_all.15 = bf16[8,4,32,768]{3,2,1,0:T(8,128)(2,1)S(1)} all-to-all(bf16[8,4,32,768]{3,2,1,0:T(8,128)(2,1)} %bitcast.113), channel_id=1, replica_groups=mesh['seq'=16,'res'=8] {'res'}, dimensions={0} | all-to-all | bytes 3145728 | tf_op jit(solution)/shard_map/all_to_all | solution.py:145
  36.1 4.4 %convolution_convert_fusion.6 = bf16[4,256,768]{2,1,0:T(8,128)(2,1)} fusion(bf16[4,256,768]{2,1,0:T(8,128)(2,1)} %copy-done.4, bf16[768,768]{1,0:T(8,128)(2,1)} %param.10), kind=kOutput, calls=%fused_computation.29 | convolution fusion | flops 1208745984 | bytes 4325376 | tf_op jit(solution)/shard_map/dot_general | solution.py:25
  40.5 2.5 %convolution_convert_fusion.7 = bf16[4,256,768]{2,1,0:T(8,128)(2,1)} fusion(bf16[4,256,768]{2,1,0:T(8,128)(2,1)S(1)} %copy-done.5, bf16[768,768]{1,0:T(8,128)(2,1)S(1)} %copy-done.8), kind=kOutput, calls=%fused_computation.30 | convolution fusion | flops 1208745984 | bytes 4325376 | tf_op jit(solution)/shard_map/dot_general | solution.py:25
  43.1 1.7 copy.98
  44.8 2.6 %copy.99 = bf16[4,256,768]{1,2,0:T(8,128)(2,1)} copy(bf16[4,256,768]{2,1,0:T(8,128)(2,1)} %convolution_convert_fusion.6) | data formatting | bytes 3145728 | tf_op jit(solution)/shard_map/convert_element_type | solution.py:150
  47.4 3.7 %convolution_bitcast_fusion.part = f32[12,32,8,256]{3,2,1,0:T(8,128)} fusion(bf16[4,256,12,64]{1,3,2,0:T(8,128)(2,1)} %bitcast.112, bf16[4,256,12,64]{1,3,2,0:T(8,128)(2,1)S(1)} %bitcast.110), kind=kOutput, calls=%fused_computation.21 | convolution fusion | flops 402653184 | bytes 6291456 | tf_op jit(solution)/shard_map/rihd,rjhd->hij/dot_general | solution.py:153
  51.1 52.7 %shard_map.91 = bf16[12,32,8,256]{3,2,1,0:T(8,128)(2,1)} custom-call(f32[12,32,8,256]{3,2,1,0:T(8,128)} %convolution_bitcast_fusion.part), custom_call_target="tpu_custom_call" | custom-call | tf_op jit(solution)/shard_map/pallas_call | solution.py:121
  103.8 2.1 fusion.16
  106.1 1.7 copy-done.3
  107.8 1.5 fusion.11
  111.0 1.6 copy.105
  112.6 29.9 %all_to_all.16 = bf16[128,4,2,768]{3,2,1,0:T(2,128)(2,1)S(1)} all-to-all(bf16[128,4,2,768]{3,2,1,0:T(2,128)(2,1)S(1)} %copy.105), channel_id=1, replica_groups=mesh['seq'=16,'res'=8] {'seq','res'}, dimensions={0} | all-to-all | bytes 3145728 | tf_op jit(solution)/shard_map/all_to_all | solution.py:162
  142.9 2.4 %copy.107 = f32[128,4,2,768]{3,2,1,0:T(2,128)S(1)} copy(f32[128,4,2,768]{3,0,2,1:T(8,128)S(1)} %copy_convert_fusion) | data formatting | bytes 6291456 | tf_op jit(solution)/shard_map/convert_element_type | solution.py:173
  147.6 2.6 %convolution_convert_fusion.1 = bf16[2,512,768]{2,1,0:T(8,128)(2,1)} fusion(bf16[2,512,768]{2,1,0:T(8,128)(2,1)S(1)} %multiply_convert_fusion, bf16[768,768]{1,0:T(8,128)(2,1)S(1)} %copy-done.10), kind=kOutput, calls=%fused_computation.24 | convolution fusion | flops 1208745984 | bytes 4325376 | tf_op jit(solution)/shard_map/dot_general | solution.py:25
  150.1 2.6 %copy.111 = bf16[2,512,768]{1,2,0:T(8,128)(2,1)} copy(bf16[2,512,768]{2,1,0:T(8,128)(2,1)} %convolution_convert_fusion.1) | data formatting | bytes 3145728 | tf_op jit(solution)/shard_map/convert_element_type | solution.py:166
  152.8 4.4 %convolution_convert_fusion.2 = bf16[2,512,768]{2,1,0:T(8,128)(2,1)} fusion(bf16[2,512,768]{2,1,0:T(8,128)(2,1)} %copy-done.6, bf16[768,768]{1,0:T(8,128)(2,1)} %param.14), kind=kOutput, calls=%fused_computation.25 | convolution fusion | flops 1208745984 | bytes 4325376 | tf_op jit(solution)/shard_map/dot_general | solution.py:25
  157.2 2.5 %convolution_convert_fusion.3 = bf16[2,512,768]{2,1,0:T(8,128)(2,1)} fusion(bf16[2,512,768]{2,1,0:T(8,128)(2,1)S(1)} %copy-done.7, bf16[768,768]{1,0:T(8,128)(2,1)S(1)} %copy-done.11), kind=kOutput, calls=%fused_computation.26 | convolution fusion | flops 1208745984 | bytes 4325376 | tf_op jit(solution)/shard_map/dot_general | solution.py:25
  159.8 2.6 %copy.109 = bf16[2,512,768]{1,2,0:T(8,128)(2,1)} copy(bf16[2,512,768]{2,1,0:T(8,128)(2,1)} %convolution_convert_fusion.3) | data formatting | bytes 3145728 | tf_op jit(solution)/shard_map/convert_element_type | solution.py:167
  162.4 2.6 %copy.110 = bf16[2,512,768]{1,2,0:T(8,128)(2,1)} copy(bf16[2,512,768]{2,1,0:T(8,128)(2,1)} %convolution_convert_fusion.2) | data formatting | bytes 3145728 | tf_op jit(solution)/shard_map/convert_element_type | solution.py:165
  165.0 14.2 %fusion.32 = (f32[2,12,512]{2,1,0:T(8,128)S(1)}, f32[2,12,512,512]{2,3,1,0:T(8,128)}) fusion(bf16[2,512,12,64]{1,3,2,0:T(8,128)(2,1)} %bitcast.116, bf16[2,512,12,64]{1,3,2,0:T(8,128)(2,1)} %bitcast.114), kind=kOutput, calls=%fused_computation.53 | convolution fusion | flops 824181248 | bytes 28360704 | tf_op jit(solution)/shard_map/sub | solution.py:169
  179.1 11.0 %fusion.12 = bf16[2,12,64,512]{3,2,1,0:T(8,128)(2,1)S(1)} fusion(bf16[2,512,12,64]{1,3,2,0:T(8,128)(2,1)} %bitcast.115, f32[2,12,512,512]{2,3,1,0:T(8,128)} %get-tuple-element.6, f32[2,12,512]{2,1,0:T(8,128)S(1)} %get-tuple-element.5), kind=kOutput, calls=%fused_computation.22 | convolution fusion | flops 818675712 | bytes 28360704 | tf_op jit(solution)/shard_map/chrs,cshd->crhd/dot_general | solution.py:170
  190.2 1.4 fusion.8
  191.8 25.8 %all_to_all.17 = bf16[16,32,2,768]{3,1,2,0:T(8,128)(2,1)S(1)} all-to-all(bf16[16,32,2,768]{3,1,2,0:T(8,128)(2,1)S(1)} %bitcast.108), channel_id=1, replica_groups=mesh['seq'=16,'res'=8] {'seq'}, dimensions={0} | all-to-all | bytes 3145728 | tf_op jit(solution)/shard_map/all_to_all | solution.py:175
  217.6 2.0 copy.115
  (47 shorter events, 11.2 us)
Async XLA Ops:
  0.0 34.0 %copy-start = (bf16[768,768]{1,0:T(8,128)(2,1)S(1)}, bf16[768,768]{1,0:T(8,128)(2,1)}, u32[]{:S(2)}) copy-start(bf16[768,768]{1,0:T(8,128)(2,1)} %param.11) | copy-start | bytes 3538948
  31.2 1.7 copy-start.2
  32.8 1.1 copy-start.4
  36.1 4.5 %copy-start.5 = (bf16[4,256,768]{2,1,0:T(8,128)(2,1)S(1)}, bf16[4,256,768]{2,1,0:T(8,128)(2,1)}, u32[]{:S(2)}) copy-start(bf16[4,256,768]{2,1,0:T(8,128)(2,1)} %copy-done.4) | copy-start | bytes 4718596
  36.1 4.4 %copy-start.8 = (bf16[768,768]{1,0:T(8,128)(2,1)S(1)}, bf16[768,768]{1,0:T(8,128)(2,1)}, u32[]{:S(2)}) copy-start(bf16[768,768]{1,0:T(8,128)(2,1)} %param.12) | copy-start | bytes 3538948
  103.8 2.3 %copy-start.9 = (bf16[768,768]{1,0:T(8,128)(2,1)S(1)}, bf16[768,768]{1,0:T(8,128)(2,1)}, u32[]{:S(2)}) copy-start(bf16[768,768]{1,0:T(8,128)(2,1)} %param.13) | copy-start | bytes 3538948
  105.9 1.9 copy-start.3
  146.1 1.5 copy-start.10
  146.4 1.1 copy-start.6
  152.8 4.4 %copy-start.7 = (bf16[2,512,768]{2,1,0:T(8,128)(2,1)S(1)}, bf16[2,512,768]{2,1,0:T(8,128)(2,1)}, u32[]{:S(2)}) copy-start(bf16[2,512,768]{2,1,0:T(8,128)(2,1)} %copy-done.6) | copy-start | bytes 4718596
  152.8 4.4 %copy-start.11 = (bf16[768,768]{1,0:T(8,128)(2,1)S(1)}, bf16[768,768]{1,0:T(8,128)(2,1)}, u32[]{:S(2)}) copy-start(bf16[768,768]{1,0:T(8,128)(2,1)} %param.16) | copy-start | bytes 3538948
  179.1 11.0 %copy-start.12 = (bf16[768,768]{1,0:T(8,128)(2,1)S(1)}, bf16[768,768]{1,0:T(8,128)(2,1)}, u32[]{:S(2)}) copy-start(bf16[768,768]{1,0:T(8,128)(2,1)} %param.17) | copy-start | bytes 3538948
  217.6 2.0 copy-start.1
